TPU v7x, 32 devices: a whole 2x2x4 slice. The times are simulated.
32 devices in a mesh: shot: 2 (over core), probe: 16 (over z, y, x).
Axes of the slice: x: 2, y: 2, z: 4, core: 2. Of those that a mesh axis runs over, the one named last changes fastest.
Arguments:
- probes: float32 [32, 256, 512], P('probe'), may hold values from -6 to 6
- coarse_sample: float32 [32, 256, 512], P('probe', 'shot'), may hold values from -6 to 6
- coefficient: float32 [256, 512], replicated, may hold values from 0.05 to 0.45
- receiver: float32 [256, 512], replicated, may hold values from 0.05 to 0.5
- checkpoints: float32 [4, 2, 256, 512], P('shot', None, 'probe'), may hold values from -6 to 6
- encodings: int32 [4, 256], P('shot'), may hold values from -1 to 1, as said below
- wavelet: float32 [3, 256], replicated, may hold values from -6 to 6
- bounds: int32 [33], replicated, may hold values from 0 to 256, as said below
Outputs:
- samples: float32 [32, 256, 512], P('probe', 'shot')
Inputs may be any that keep to these rules, and one draw needn't show every extreme that they name: `encodings`: every entry is -1 or 1. bounds[0] = 0 and bounds[32] = 256; the entries rise strictly; blocks 2 i and 2 i + 1 together hold exactly 16 rows.
All inputs are finite; a program needn't handle non-finite values.
Results may differ from a plain program's by a relative error of at most 0.000094.
Values sent between devices are 32-bit elements; how exact they have to be, the bound alone decides.
A program may use at most 128 MiB of HBM per device.

v0:
```python
import jax
import jax.numpy as jnp
from jax import lax
from jax.sharding import PartitionSpec as P

NZ = 512
NSHOT = 256
NT = 4


def laplace(values):
    pad_width = [(0, 0)] * (values.ndim - 2) + [(1, 1), (1, 1)]
    padded = jnp.pad(values, pad_width)
    return (
        padded[..., 2:, 1:-1]
        + padded[..., :-2, 1:-1]
        + padded[..., 1:-1, 2:]
        + padded[..., 1:-1, :-2]
        - 4.0 * values
    )


def shot_sources(encodings, wavelet):
    columns = jnp.arange(NZ)
    spacing = NZ // NSHOT
    position = jnp.arange(NSHOT) * NZ // NSHOT + spacing // 2
    onehot = (position[:, None] == columns[None, :]).astype(jnp.float32)
    amplitude = encodings.astype(jnp.float32)[:, None, :] * wavelet[None, :, :]
    return jnp.einsum("stk,kz->stz", amplitude, onehot, precision=lax.Precision.HIGHEST)


def block_parity(row_index, bounds):
    inner = bounds[1:-1]
    return jnp.sum((row_index[:, None] >= inner[None, :]).astype(jnp.int32), axis=1) % 2


def hessian_term(vectors, levels, coefficient, weight_square):
    before = jnp.zeros_like(vectors)
    current = jnp.zeros_like(vectors)
    deltas = []
    for moment in range(NT):
        following = (
            2.0 * current - before + coefficient * laplace(current) + vectors * levels[moment]
        )
        before, current = (current, following)
        deltas.append(following)
    upcoming = jnp.zeros_like(vectors)
    beyond = jnp.zeros_like(vectors)
    gradient = jnp.zeros_like(vectors)
    for moment in range(NT, 0, -1):
        adjoint = (
            weight_square * deltas[moment - 1]
            + 2.0 * upcoming
            + laplace(coefficient * upcoming)
            - beyond
        )
        gradient = gradient + levels[moment - 1] * adjoint
        beyond, upcoming = (upcoming, adjoint)
    return gradient


def on_device(
    probes, coarse_sample, coefficient, receiver, checkpoints, encodings, wavelet, bounds
):
    num_rows = probes.shape[1]
    source_at = num_rows // 2
    sources = shot_sources(encodings, wavelet)
    colour = jnp.arange(probes.shape[0]) % 2
    parity_all = block_parity(jnp.arange(num_rows), bounds)
    support = (parity_all[None, :] == colour[:, None]).astype(jnp.float32)
    vectors = probes * support[:, :, None]
    weight_square = receiver * receiver
    accumulated = jnp.zeros_like(probes)
    for member in range(checkpoints.shape[0]):
        stored = lax.all_gather(checkpoints[member], "probe", axis=1, tiled=True)
        at_source = (jnp.arange(num_rows) == source_at).astype(jnp.float32)[:, None]
        before = stored[0]
        current = stored[1]
        history = [current]
        for moment in range(NT - 1):
            following = (
                2.0 * current
                - before
                + coefficient * laplace(current)
                + at_source * sources[member, moment][None, :]
            )
            before, current = (current, following)
            history.append(current)
        levels = jnp.stack(history)
        accumulated = accumulated + hessian_term(vectors, levels, coefficient, weight_square)
    out_rows = coarse_sample.shape[1]
    summed = lax.psum(accumulated, "shot")
    share = lax.dynamic_slice_in_dim(summed, lax.axis_index("shot") * out_rows, out_rows, 1)
    row_out = lax.axis_index("shot") * out_rows + jnp.arange(out_rows)
    keep = (block_parity(row_out, bounds)[None, :] != colour[:, None]).astype(jnp.float32)
    return keep[:, :, None] * (share - coarse_sample)


def solution(mesh):
    return jax.shard_map(
        on_device,
        mesh=mesh,
        in_specs=(
            P("probe", None, None),
            P("probe", "shot", None),
            P(),
            P(),
            P("shot", None, "probe", None),
            P("shot", None),
            P(),
            P(),
        ),
        out_specs=P("probe", "shot", None),
        check_vma=False,
    )
```

profile of v0, /device:TPU:0, one launch (start us, length us, event | category | flops | bytes accessed | tf_op | source)
XLA Modules:
  0.0 186.1 jit_solution(16880601217154744731)
XLA Ops:
  6.5 1.5 fusion.153
  8.1 0.7 all-gather.5.cloned.1.call-update
  8.9 0.7 convert_element_type.69
  9.6 0.7 slice.296
  10.3 1.4 mul.554
  12.3 55.9 %all-gather.7.cloned.1.call-done = f32[1,2,256,512]{3,2,1,0:T(8,128)} async-done(((f32[1,2,16,512]{3,2,1,0:T(8,128)}), f32[1,2,256,512]{3,2,1,0:T(8,128)}) %all-gather.7.cloned.1.call-update) | async-done | bytes 1048592 | tf_op jit(solution)/shard_map/all_gather | solution.py:75
  68.2 1.2 slice_bitcast_fusion.1
  69.4 55.8 %all-gather.5.cloned.1.call-done = f32[1,2,256,512]{3,2,1,0:T(8,128)} async-done(((f32[1,2,16,512]{3,2,1,0:T(8,128)}), f32[1,2,256,512]{3,2,1,0:T(8,128)}) %all-gather.5.cloned.1.call-update) | async-done | bytes 1048592 | tf_op jit(solution)/shard_map/all_gather | solution.py:75
  125.2 1.1 slice_bitcast_fusion.3
  126.3 1.9 %fusion.116 = (f32[256,512]{1,0:T(8,128)S(1)}, f32[256,512]{1,0:T(8,128)S(1)}) fusion(f32[256,512]{1,0:T(8,128)S(1)} %copy-done, f32[256,512]{1,0:T(8,128)S(1)} %slice_bitcast_fusion.1, f32[1,2,256,512]{3,2,1,0:T(8,128)S(1)} %copy-done.20, f32[512]{0:T(512)S(1)} %bitcast.33, f32[256]{0:T(256)S(1)} %compare_convert_fusion.1, f32[512]{0:T(512)S(1)} %bitcast.34, ...), kind=kLoop, calls=%fused_computation.198 | loop fusion | flops 2883584 | bytes 3675136 | tf_op jit(solution)/shard_map/add | solution.py:82
  128.2 0.8 fusion.123
  129.2 1.1 fusion.130
  130.3 0.4 copy-done.1
  131.1 0.8 fusion.49
  131.8 1.5 fusion.56
  133.3 0.9 fusion.13
  134.3 0.3 fusion.109
  134.6 3.2 %broadcast_multiply_fusion.2 = (f32[2,256,512]{2,1,0:T(8,128)S(1)}, f32[2,256,512]{2,1,0:T(8,128)S(1)}, f32[2,256,512]{2,1,0:T(8,128)}, f32[2,256,512]{2,1,0:T(8,128)S(1)}) fusion(f32[256,512]{1,0:T(8,128)S(1)} %copy-done, f32[256,512]{1,0:T(8,128)S(1)} %fusion.109, f32[256,512]{1,0:T(8,128)S(1)} %get-tuple-element.25, f32[2,256,512]{2,1,0:T(8,128)S(1)} %copy-done.1, ...), kind=kLoop, calls=%fused_computation.226 | loop fusion | flops 7602176 | bytes 12060672 | tf_op jit(solution)/shard_map/mul | solution.py:54
  137.9 2.2 %broadcast_multiply_fusion.1 = (f32[2,256,512]{2,1,0:T(8,128)}, f32[2,256,512]{2,1,0:T(8,128)}) fusion(f32[256,512]{1,0:T(8,128)S(1)} %copy-done, f32[2,256,512]{2,1,0:T(8,128)S(1)} %get-tuple-element.9, f32[2,256,512]{2,1,0:T(8,128)S(1)} %get-tuple-element.10, f32[2,256,512]{2,1,0:T(8,128)S(1)} %get-tuple-element.19, f32[256,512]{1,0:T(8,128)S(1)} %mul.554), kind=kLoop, calls=%fused_computation.225 | loop fusion | flops 2621440 | bytes 6291456 | tf_op jit(solution)/shard_map/mul | solution.py:54
  140.0 9.3 %broadcast_multiply_fusion = (f32[2,256,512]{2,1,0:T(8,128)}, f32[2,256,512]{2,1,0:T(8,128)}, f32[2,256,512]{2,1,0:T(8,128)}, f32[2,256,512]{2,1,0:T(8,128)}) fusion(f32[256,512]{1,0:T(8,128)S(1)} %copy-done, f32[2,256,512]{2,1,0:T(8,128)S(1)} %get-tuple-element.10, f32[2,256,512]{2,1,0:T(8,128)} %get-tuple-element.7, f32[2,256,512]{2,1,0:T(8,128)} %get-tuple-element.8, ...), kind=kLoop, calls=%fused_computation.224 | loop fusion | flops 5505024 | bytes 12582912 | tf_op jit(solution)/shard_map/mul | solution.py:54
  149.4 4.6 %broadcast_multiply_fusion.3 = (f32[2,256,512]{2,1,0:T(8,128)S(1)}, f32[2,256,512]{2,1,0:T(8,128)S(1)}) fusion(f32[256,512]{1,0:T(8,128)S(1)} %copy-done, f32[2,256,512]{2,1,0:T(8,128)S(1)} %get-tuple-element.18, f32[2,256,512]{2,1,0:T(8,128)} %get-tuple-element.23, f32[2,256,512]{2,1,0:T(8,128)} %get-tuple-element.24, ...), kind=kLoop, calls=%fused_computation.227 | loop fusion | flops 2883584 | bytes 7340032 | tf_op jit(solution)/shard_map/mul | solution.py:54
  154.2 4.9 %fusion.42 = f32[2,256,512]{2,1,0:T(8,128)} fusion(f32[2,256,512]{2,1,0:T(8,128)S(1)} %copy-done.4, f32[2,256,512]{2,1,0:T(8,128)S(1)} %get-tuple-element.11, f32[2,256,512]{2,1,0:T(8,128)S(1)} %copy-done.6, f32[2,256,512]{2,1,0:T(8,128)S(1)} %copy-done.19, f32[2,256,512]{2,1,0:T(8,128)} %get-tuple-element.6, f32[2,256,512]{2,1,0:T(8,128)S(1)} %get-tuple-element.21, ...), kind=kLoop, calls=%fused_computation.94 | loop fusion | flops 9175040 | bytes 16252928 | tf_op jit(solution)/shard_map/add | solution.py:90
  159.4 18.3 %all-reduce.22.cloned.1.call-done = f32[2,256,512]{2,1,0:T(8,128)} async-done(((f32[2,256,512]{2,1,0:T(8,128)}), f32[2,256,512]{2,1,0:T(8,128)}) %all-reduce.22.cloned.1.call-update) | async-done | bytes 1048592 | tf_op jit(solution)/shard_map/psum | solution.py:92
  177.6 1.9 %subtract_multiply_fusion = f32[2,128,512]{2,1,0:T(8,128)} fusion(f32[2,128,512]{2,1,0:T(8,128)S(1)} %copy-done.22, f32[2,256,512]{2,1,0:T(8,128)} %all-reduce.22.cloned.1.call-done, s32[]{:T(128)S(6)} %select_n.49, f32[2,128]{1,0:T(2,128)S(1)} %compare_convert_fusion.2), kind=kLoop, calls=%fused_computation.223 | loop fusion | flops 262144 | bytes 1573892 | tf_op jit(solution)/shard_map/mul | solution.py:96
  (66 shorter events, 1.4 us)
Async XLA Ops:
  6.5 5.4 %copy-start.23 = (f32[3,256]{1,0:T(4,128)S(1)}, f32[3,256]{1,0:T(4,128)}, u32[]{:S(2)}) copy-start(f32[3,256]{1,0:T(4,128)} %param.14) | copy-start | bytes 9220
  6.5 61.6 %all-gather.7.cloned.1.call-start = ((), (), s32[]{:S(2)}) async-start(), calls=%async_computation.2 | async-start | bytes 1114112 | tf_op jit(solution)/shard_map/all_gather | solution.py:75
  8.1 117.1 %all-gather.5.cloned.1.call-start = ((), (), s32[]{:S(2)}) async-start(), calls=%async_computation.1 | async-start | bytes 1114112 | tf_op jit(solution)/shard_map/all_gather | solution.py:75
  8.8 168.8 %all-reduce.22.cloned.1.call-start = ((), (), s32[]{:S(2)}) async-start(), calls=%async_computation | async-start | bytes 2097152 | tf_op jit(solution)/shard_map/psum | solution.py:92
  12.2 114.0 %copy-start = (f32[256,512]{1,0:T(8,128)S(1)}, f32[256,512]{1,0:T(8,128)}, u32[]{:S(2)}) copy-start(f32[256,512]{1,0:T(8,128)} %param.10) | copy-start | bytes 1572868
  68.2 58.1 %copy-start.20 = (f32[1,2,256,512]{3,2,1,0:T(8,128)S(1)}, f32[1,2,256,512]{3,2,1,0:T(8,128)}, u32[]{:S(2)}) copy-start(f32[1,2,256,512]{3,2,1,0:T(8,128)} %all-gather.7.cloned.1.call-done) | copy-start | bytes 3145732
  69.3 61.0 %copy-start.7 = (f32[256,512]{1,0:T(8,128)}, f32[256,512]{1,0:T(8,128)S(1)}, u32[]{:S(2)}) copy-start(f32[256,512]{1,0:T(8,128)S(1)} %slice_bitcast_fusion.1) | copy-start | bytes 1572868
  126.2 4.1 %copy-start.9 = (f32[256,512]{1,0:T(8,128)}, f32[256,512]{1,0:T(8,128)S(1)}, u32[]{:S(2)}) copy-start(f32[256,512]{1,0:T(8,128)S(1)} %slice_bitcast_fusion.3) | copy-start | bytes 1572868
  128.2 2.8 %copy-start.2 = (f32[256,512]{1,0:T(8,128)}, f32[256,512]{1,0:T(8,128)S(1)}, u32[]{:S(2)}) copy-start(f32[256,512]{1,0:T(8,128)S(1)} %get-tuple-element.29) | copy-start | bytes 1572868
  129.1 4.2 %copy-start.13 = (f32[256,512]{1,0:T(8,128)}, f32[256,512]{1,0:T(8,128)S(1)}, u32[]{:S(2)}) copy-start(f32[256,512]{1,0:T(8,128)S(1)} %get-tuple-element.28) | copy-start | bytes 1572868
  130.3 4.3 %copy-start.15 = (f32[256,512]{1,0:T(8,128)}, f32[256,512]{1,0:T(8,128)S(1)}, u32[]{:S(2)}) copy-start(f32[256,512]{1,0:T(8,128)S(1)} %get-tuple-element.25) | copy-start | bytes 1572868
  130.3 4.3 %copy-start.17 = (f32[256,512]{1,0:T(8,128)}, f32[256,512]{1,0:T(8,128)S(1)}, u32[]{:S(2)}) copy-start(f32[256,512]{1,0:T(8,128)S(1)} %get-tuple-element.26) | copy-start | bytes 1572868
  134.3 3.6 %copy-start.5 = (f32[2,256,512]{2,1,0:T(8,128)}, f32[2,256,512]{2,1,0:T(8,128)S(1)}, u32[]{:S(2)}) copy-start(f32[2,256,512]{2,1,0:T(8,128)S(1)} %fusion.13) | copy-start | bytes 3145732
  149.4 4.7 %copy-start.3 = (f32[256,512]{1,0:T(8,128)S(1)}, f32[256,512]{1,0:T(8,128)}, u32[]{:S(2)}) copy-start(f32[256,512]{1,0:T(8,128)} %copy-done.2) | copy-start | bytes 1572868
  149.4 4.7 %copy-start.4 = (f32[2,256,512]{2,1,0:T(8,128)S(1)}, f32[2,256,512]{2,1,0:T(8,128)}, u32[]{:S(2)}) copy-start(f32[2,256,512]{2,1,0:T(8,128)} %get-tuple-element.24) | copy-start | bytes 3145732
  149.4 4.7 %copy-start.6 = (f32[2,256,512]{2,1,0:T(8,128)S(1)}, f32[2,256,512]{2,1,0:T(8,128)}, u32[]{:S(2)}) copy-start(f32[2,256,512]{2,1,0:T(8,128)} %get-tuple-element.8) | copy-start | bytes 3145732
  149.4 4.7 %copy-start.8 = (f32[256,512]{1,0:T(8,128)S(1)}, f32[256,512]{1,0:T(8,128)}, u32[]{:S(2)}) copy-start(f32[256,512]{1,0:T(8,128)} %copy-done.7) | copy-start | bytes 1572868
  149.4 4.7 %copy-start.10 = (f32[256,512]{1,0:T(8,128)S(1)}, f32[256,512]{1,0:T(8,128)}, u32[]{:S(2)}) copy-start(f32[256,512]{1,0:T(8,128)} %copy-done.9) | copy-start | bytes 1572868
  149.4 4.7 %copy-start.12 = (f32[256,512]{1,0:T(8,128)S(1)}, f32[256,512]{1,0:T(8,128)}, u32[]{:S(2)}) copy-start(f32[256,512]{1,0:T(8,128)} %copy-done.11) | copy-start | bytes 1572868
  149.4 4.7 %copy-start.14 = (f32[256,512]{1,0:T(8,128)S(1)}, f32[256,512]{1,0:T(8,128)}, u32[]{:S(2)}) copy-start(f32[256,512]{1,0:T(8,128)} %copy-done.13) | copy-start | bytes 1572868
  149.4 4.7 %copy-start.16 = (f32[256,512]{1,0:T(8,128)S(1)}, f32[256,512]{1,0:T(8,128)}, u32[]{:S(2)}) copy-start(f32[256,512]{1,0:T(8,128)} %copy-done.15) | copy-start | bytes 1572868
  149.4 4.7 %copy-start.18 = (f32[256,512]{1,0:T(8,128)S(1)}, f32[256,512]{1,0:T(8,128)}, u32[]{:S(2)}) copy-start(f32[256,512]{1,0:T(8,128)} %copy-done.17) | copy-start | bytes 1572868
  149.4 4.8 %copy-start.19 = (f32[2,256,512]{2,1,0:T(8,128)S(1)}, f32[2,256,512]{2,1,0:T(8,128)}, u32[]{:S(2)}) copy-start(f32[2,256,512]{2,1,0:T(8,128)} %get-tuple-element.5) | copy-start | bytes 3145732
  159.2 18.5 %copy-start.22 = (f32[2,128,512]{2,1,0:T(8,128)S(1)}, f32[2,128,512]{2,1,0:T(8,128)}, u32[]{:S(2)}) copy-start(f32[2,128,512]{2,1,0:T(8,128)} %param.9) | copy-start | bytes 1572868
  (3 other events, 6.2 us)
Sparse Core Ops, SparseCore 0:
  10.1 58.0 all-gather.6
  70.9 54.1 all-gather.4
  159.3 18.2 all-reduce.21
where the time goes:
time: 187 us; the launch traced here: 186 us
  waiting for transfers between devices  131 us (70%)
  other arithmetic  36.4 us (19%)
  between operations  13.5 us (7%)
  local copies, waits for them, and re-layouts  5.07 us (3%)
    all_gather x2, waiting for transfers between devices, on_device(): stored = lax.all_gather(checkpoints[member], 'probe', axis=1, tiled=True)  112 us
    mul x4, other arithmetic, hessian_term(): coefficient * upcoming  19.3 us
    psum x1, waiting for transfers between devices, on_device(): summed = lax.psum(accumulated, 'shot')  18.3 us
    add x1, other arithmetic, on_device(): accumulated + hessian_term(vectors, levels, coefficient, weight_square)  4.94 us
    add x3, other arithmetic, on_device(): 2.0 * current - before + coefficient * laplace(current)  3.89 us
  transfers between devices with their start and end apart: 3, of which 3 were waited for; matrix products, arithmetic and copies ran while one was open for 3% of the time, Pallas kernels for 0%

commit v1 on v0

--- a/solution.py
+++ b/solution.py
@@ -72,7 +72,29 @@
     weight_square = receiver * receiver
     accumulated = jnp.zeros_like(probes)
     for member in range(checkpoints.shape[0]):
-        stored = lax.all_gather(checkpoints[member], "probe", axis=1, tiled=True)
+        ways, here, step = (
+            lax.axis_size("probe"),
+            lax.axis_index("probe"),
+            checkpoints[member].shape[1],
+        )
+        lengths = [n * ways if d == 1 else n for d, n in enumerate(checkpoints[member].shape)]
+        full = lax.dynamic_update_slice_in_dim(
+            jnp.zeros(lengths, checkpoints[member].dtype), checkpoints[member], here * step, axis=1
+        )
+        going_up = going_down = checkpoints[member]
+        for far in range(1, ways // 2 + 1):
+            going_up = lax.ppermute(going_up, "probe", [(d, (d + 1) % ways) for d in range(ways)])
+            full = lax.dynamic_update_slice_in_dim(
+                full, going_up, (here - far) % ways * step, axis=1
+            )
+            if 2 * far < ways:
+                going_down = lax.ppermute(
+                    going_down, "probe", [(d, (d - 1) % ways) for d in range(ways)]
+                )
+                full = lax.dynamic_update_slice_in_dim(
+                    full, going_down, (here + far) % ways * step, axis=1
+                )
+        stored = full
         at_source = (jnp.arange(num_rows) == source_at).astype(jnp.float32)[:, None]
         before = stored[0]
         current = stored[1]

time: 187 us -> 173 us (0.925)
  waiting for transfers between devices: 131 us -> 23.8 us
  starting transfers between devices: 0.08 us -> 80.4 us
  local copies, waits for them, and re-layouts: 5.07 us -> 16.4 us
    all_gather x2 -> x0, waiting for transfers between devices: 112 us -> none  [on_device(): stored = lax.all_gather(checkpoints[member], 'probe', axis=1, tiled=True)]
    ppermute x0 -> x30, starting transfers between devices: none -> 80.4 us  [the longest x14 77 us: on_device(): lax.ppermute(going_down, 'probe', [(d, (d - 1) % ways) for d in range(way...]
    dynamic_update_slice x0 -> x32, local copies, waits for them, and re-layouts: none -> 10.4 us  [the longest x16 5.16 us: on_device(): lax.dynamic_update_slice_in_dim(full, going_up, (here - far) % ways * ste...]
    ppermute x0 -> x30, waiting for transfers between devices: none -> 7.46 us  [the longest x16 7.43 us: on_device(): lax.ppermute(going_up, 'probe', [(d, (d + 1) % ways) for d in range(ways)])]
    psum x1, waiting for transfers between devices: 18.3 us -> 16.3 us  [on_device(): summed = lax.psum(accumulated, 'shot')]
  transfers between devices with their start and end apart: 3 -> 31, of which waited for: 3 -> 3; matrix products, arithmetic and copies ran while one was open for 3% -> 9% of each run, Pallas kernels for 0% -> 0%
where the time goes in v1:
time: 173 us
  starting transfers between devices  80.4 us (46%)
  other arithmetic  37 us (21%)
  waiting for transfers between devices  23.8 us (14%)
  local copies, waits for them, and re-layouts  16.4 us (9%)
  between operations  14.2 us (8%)
    ppermute x14, starting transfers between devices, on_device(): lax.ppermute(going_down, 'probe', [(d, (d - 1) % ways) for d in range(way...  77 us
    mul x4, other arithmetic, hessian_term(): coefficient * upcoming  19.4 us
    psum x1, waiting for transfers between devices, on_device(): summed = lax.psum(accumulated, 'shot')  16.3 us
    ppermute x16, waiting for transfers between devices, on_device(): lax.ppermute(going_up, 'probe', [(d, (d + 1) % ways) for d in range(ways)])  7.43 us
    dynamic_update_slice x16, local copies, waits for them, and re-layouts, on_device(): lax.dynamic_update_slice_in_dim(full, going_up, (here - far) % ways * ste...  5.16 us
    add x1, other arithmetic, on_device(): accumulated + hessian_term(vectors, levels, coefficient, weight_square)  4.98 us
    add x3, other arithmetic, on_device(): 2.0 * current - before + coefficient * laplace(current)  4.79 us
    dynamic_update_slice x14, local copies, waits for them, and re-layouts, on_device(): lax.dynamic_update_slice_in_dim(full, going_down, (here + far) % ways * s...  4.57 us
  transfers between devices with their start and end apart: 31, of which 3 were waited for; matrix products, arithmetic and copies ran while one was open for 9% of the time, Pallas kernels for 0%

profile of v1, /device:TPU:0, one launch (start us, length us, event | category | flops | bytes accessed | tf_op | source)
XLA Modules:
  0.0 172.9 jit_solution(16138943688493683275)
XLA Ops:
  7.5 3.0 %collective-permute-start.15 = (f32[2,16,512]{2,1,0:T(8,128)S(1)}, f32[2,16,512]{2,1,0:T(8,128)S(1)}, u32[]{:S(2)}, u32[]{:S(2)}) collective-permute-start(f32[2,16,512]{2,1,0:T(8,128)S(1)} %get-tuple-element.32), channel_id=1, source_target_pairs={{0,1},{1,2},{2,3},{3,4},{4,5},{5,6},{6,7},{7,8},{8,9},{9,10},{10,1... | collective-permute-start | bytes 196616 | tf_op jit(solution)/shard_map/ppermute | solution.py:86
  10.5 4.1 %collective-permute-start.16 = (f32[2,16,512]{2,1,0:T(8,128)S(1)}, f32[2,16,512]{2,1,0:T(8,128)S(1)}, u32[]{:S(2)}, u32[]{:S(2)}) collective-permute-start(f32[2,16,512]{2,1,0:T(8,128)S(1)} %get-tuple-element.32), channel_id=1, source_target_pairs={{0,15},{1,0},{2,1},{3,2},{4,3},{5,4},{6,5},{7,6},{8,7},{9,8},{10,9... | collective-permute-start | bytes 196616 | tf_op jit(solution)/shard_map/ppermute | solution.py:91
  14.6 5.6 %collective-permute-start.1 = (f32[2,16,512]{2,1,0:T(8,128)S(1)}, f32[2,16,512]{2,1,0:T(8,128)S(1)}, u32[]{:S(2)}, u32[]{:S(2)}) collective-permute-start(f32[2,16,512]{2,1,0:T(8,128)S(1)} %get-tuple-element.33), channel_id=1, source_target_pairs={{0,15},{1,0},{2,1},{3,2},{4,3},{5,4},{6,5},{7,6},{8,7},{9,8},{10,9... | collective-permute-start | bytes 196616 | tf_op jit(solution)/shard_map/ppermute | solution.py:91
  25.0 5.6 %collective-permute-start.18 = (f32[2,16,512]{2,1,0:T(8,128)S(1)}, f32[2,16,512]{2,1,0:T(8,128)S(1)}, u32[]{:S(2)}, u32[]{:S(2)}) collective-permute-start(f32[2,16,512]{2,1,0:T(8,128)S(1)} %collective-permute-done.16), channel_id=1, source_target_pairs={{0,15},{1,0},{2,1},{3,2},{4,3},{5,4},{6,5},{7,6},{8,7},{9,8},{10,9... | collective-permute-start | bytes 196616 | tf_op jit(solution)/shard_map/ppermute | solution.py:91
  30.6 5.6 %collective-permute-start.3 = (f32[2,16,512]{2,1,0:T(8,128)S(1)}, f32[2,16,512]{2,1,0:T(8,128)S(1)}, u32[]{:S(2)}, u32[]{:S(2)}) collective-permute-start(f32[2,16,512]{2,1,0:T(8,128)S(1)} %collective-permute-done.1), channel_id=1, source_target_pairs={{0,15},{1,0},{2,1},{3,2},{4,3},{5,4},{6,5},{7,6},{8,7},{9,8},{10,9... | collective-permute-start | bytes 196616 | tf_op jit(solution)/shard_map/ppermute | solution.py:91
  37.6 5.6 %collective-permute-start.20 = (f32[2,16,512]{2,1,0:T(8,128)S(1)}, f32[2,16,512]{2,1,0:T(8,128)S(1)}, u32[]{:S(2)}, u32[]{:S(2)}) collective-permute-start(f32[2,16,512]{2,1,0:T(8,128)S(1)} %collective-permute-done.18), channel_id=1, source_target_pairs={{0,15},{1,0},{2,1},{3,2},{4,3},{5,4},{6,5},{7,6},{8,7},{9,8},{10,9... | collective-permute-start | bytes 196616 | tf_op jit(solution)/shard_map/ppermute | solution.py:91
  43.2 5.6 %collective-permute-start.5 = (f32[2,16,512]{2,1,0:T(8,128)S(1)}, f32[2,16,512]{2,1,0:T(8,128)S(1)}, u32[]{:S(2)}, u32[]{:S(2)}) collective-permute-start(f32[2,16,512]{2,1,0:T(8,128)S(1)} %collective-permute-done.3), channel_id=1, source_target_pairs={{0,15},{1,0},{2,1},{3,2},{4,3},{5,4},{6,5},{7,6},{8,7},{9,8},{10,9... | collective-permute-start | bytes 196616 | tf_op jit(solution)/shard_map/ppermute | solution.py:91
  50.2 5.6 %collective-permute-start.22 = (f32[2,16,512]{2,1,0:T(8,128)S(1)}, f32[2,16,512]{2,1,0:T(8,128)S(1)}, u32[]{:S(2)}, u32[]{:S(2)}) collective-permute-start(f32[2,16,512]{2,1,0:T(8,128)S(1)} %collective-permute-done.20), channel_id=1, source_target_pairs={{0,15},{1,0},{2,1},{3,2},{4,3},{5,4},{6,5},{7,6},{8,7},{9,8},{10,9... | collective-permute-start | bytes 196616 | tf_op jit(solution)/shard_map/ppermute | solution.py:91
  55.8 5.6 %collective-permute-start.7 = (f32[2,16,512]{2,1,0:T(8,128)S(1)}, f32[2,16,512]{2,1,0:T(8,128)S(1)}, u32[]{:S(2)}, u32[]{:S(2)}) collective-permute-start(f32[2,16,512]{2,1,0:T(8,128)S(1)} %collective-permute-done.5), channel_id=1, source_target_pairs={{0,15},{1,0},{2,1},{3,2},{4,3},{5,4},{6,5},{7,6},{8,7},{9,8},{10,9... | collective-permute-start | bytes 196616 | tf_op jit(solution)/shard_map/ppermute | solution.py:91
  62.8 5.6 %collective-permute-start.24 = (f32[2,16,512]{2,1,0:T(8,128)S(1)}, f32[2,16,512]{2,1,0:T(8,128)S(1)}, u32[]{:S(2)}, u32[]{:S(2)}) collective-permute-start(f32[2,16,512]{2,1,0:T(8,128)S(1)} %collective-permute-done.22), channel_id=1, source_target_pairs={{0,15},{1,0},{2,1},{3,2},{4,3},{5,4},{6,5},{7,6},{8,7},{9,8},{10,9... | collective-permute-start | bytes 196616 | tf_op jit(solution)/shard_map/ppermute | solution.py:91
  68.5 5.6 %collective-permute-start.9 = (f32[2,16,512]{2,1,0:T(8,128)S(1)}, f32[2,16,512]{2,1,0:T(8,128)S(1)}, u32[]{:S(2)}, u32[]{:S(2)}) collective-permute-start(f32[2,16,512]{2,1,0:T(8,128)S(1)} %collective-permute-done.7), channel_id=1, source_target_pairs={{0,15},{1,0},{2,1},{3,2},{4,3},{5,4},{6,5},{7,6},{8,7},{9,8},{10,9... | collective-permute-start | bytes 196616 | tf_op jit(solution)/shard_map/ppermute | solution.py:91
  75.5 5.6 %collective-permute-start.26 = (f32[2,16,512]{2,1,0:T(8,128)S(1)}, f32[2,16,512]{2,1,0:T(8,128)S(1)}, u32[]{:S(2)}, u32[]{:S(2)}) collective-permute-start(f32[2,16,512]{2,1,0:T(8,128)S(1)} %collective-permute-done.24), channel_id=1, source_target_pairs={{0,15},{1,0},{2,1},{3,2},{4,3},{5,4},{6,5},{7,6},{8,7},{9,8},{10,9... | collective-permute-start | bytes 196616 | tf_op jit(solution)/shard_map/ppermute | solution.py:91
  81.1 5.6 %collective-permute-start.11 = (f32[2,16,512]{2,1,0:T(8,128)S(1)}, f32[2,16,512]{2,1,0:T(8,128)S(1)}, u32[]{:S(2)}, u32[]{:S(2)}) collective-permute-start(f32[2,16,512]{2,1,0:T(8,128)S(1)} %collective-permute-done.9), channel_id=1, source_target_pairs={{0,15},{1,0},{2,1},{3,2},{4,3},{5,4},{6,5},{7,6},{8,7},{9,8},{10,9... | collective-permute-start | bytes 196616 | tf_op jit(solution)/shard_map/ppermute | solution.py:91
  88.1 5.6 %collective-permute-start.28 = (f32[2,16,512]{2,1,0:T(8,128)S(1)}, f32[2,16,512]{2,1,0:T(8,128)S(1)}, u32[]{:S(2)}, u32[]{:S(2)}) collective-permute-start(f32[2,16,512]{2,1,0:T(8,128)S(1)} %collective-permute-done.26), channel_id=1, source_target_pairs={{0,15},{1,0},{2,1},{3,2},{4,3},{5,4},{6,5},{7,6},{8,7},{9,8},{10,9... | collective-permute-start | bytes 196616 | tf_op jit(solution)/shard_map/ppermute | solution.py:91
  93.7 5.6 %collective-permute-start.13 = (f32[2,16,512]{2,1,0:T(8,128)S(1)}, f32[2,16,512]{2,1,0:T(8,128)S(1)}, u32[]{:S(2)}, u32[]{:S(2)}) collective-permute-start(f32[2,16,512]{2,1,0:T(8,128)S(1)} %collective-permute-done.11), channel_id=1, source_target_pairs={{0,15},{1,0},{2,1},{3,2},{4,3},{5,4},{6,5},{7,6},{8,7},{9,8},{10,9... | collective-permute-start | bytes 196616 | tf_op jit(solution)/shard_map/ppermute | solution.py:91
  102.9 6.5 %collective-permute-done.14 = f32[2,16,512]{2,1,0:T(8,128)S(1)} collective-permute-done((f32[2,16,512]{2,1,0:T(8,128)S(1)}, f32[2,16,512]{2,1,0:T(8,128)S(1)}, u32[]{:S(2)}, u32[]{:S(2)}) %collective-permute-start.14) | collective-permute-done | bytes 65568 | tf_op jit(solution)/shard_map/ppermute | solution.py:86
  111.3 2.1 %fusion.120 = (f32[256,512]{1,0:T(8,128)S(1)}, f32[256,512]{1,0:T(8,128)S(1)}) fusion(f32[256,512]{1,0:T(8,128)S(1)} %copy-done, f32[256,512]{1,0:T(8,128)S(1)} %slice_bitcast_fusion.1, f32[2,256,512]{2,1,0:T(8,128)S(1)} %constant_dynamic-update-slice_fusion, f32[512]{0:T(512)S(1)} %bitcast.39, f32[256]{0:T(256)S(1)} %compare_convert_fusion.1, ...), kind=kLoop, calls=%fused_computation.202 | loop fusion | flops 2883584 | bytes 3675136 | tf_op jit(solution)/shard_map/add | solution.py:104
  122.9 3.3 %broadcast_multiply_fusion.2 = (f32[2,256,512]{2,1,0:T(8,128)S(1)}, f32[2,256,512]{2,1,0:T(8,128)S(1)}, f32[2,256,512]{2,1,0:T(8,128)}, f32[2,256,512]{2,1,0:T(8,128)S(1)}) fusion(f32[256,512]{1,0:T(8,128)S(1)} %copy-done, f32[256,512]{1,0:T(8,128)S(1)} %fusion.113, f32[256,512]{1,0:T(8,128)S(1)} %get-tuple-element.25, f32[2,256,512]{2,1,0:T(8,128)S(1)} %copy-done.1, ...), kind=kLoop, calls=%fused_computation.226 | loop fusion | flops 7602176 | bytes 12060672 | tf_op jit(solution)/shard_map/mul | solution.py:54
  126.2 2.1 %broadcast_multiply_fusion.1 = (f32[2,256,512]{2,1,0:T(8,128)}, f32[2,256,512]{2,1,0:T(8,128)}) fusion(f32[256,512]{1,0:T(8,128)S(1)} %copy-done, f32[2,256,512]{2,1,0:T(8,128)S(1)} %get-tuple-element.9, f32[2,256,512]{2,1,0:T(8,128)S(1)} %get-tuple-element.10, f32[2,256,512]{2,1,0:T(8,128)S(1)} %get-tuple-element.21, f32[256,512]{1,0:T(8,128)S(1)} %mul.631), kind=kLoop, calls=%fused_computation.225 | loop fusion | flops 2621440 | bytes 6291456 | tf_op jit(solution)/shard_map/mul | solution.py:54
  128.3 9.4 %broadcast_multiply_fusion = (f32[2,256,512]{2,1,0:T(8,128)}, f32[2,256,512]{2,1,0:T(8,128)}, f32[2,256,512]{2,1,0:T(8,128)}, f32[2,256,512]{2,1,0:T(8,128)}) fusion(f32[256,512]{1,0:T(8,128)S(1)} %copy-done, f32[2,256,512]{2,1,0:T(8,128)S(1)} %get-tuple-element.10, f32[2,256,512]{2,1,0:T(8,128)} %get-tuple-element.7, f32[2,256,512]{2,1,0:T(8,128)} %get-tuple-element.8, ...), kind=kLoop, calls=%fused_computation.224 | loop fusion | flops 5505024 | bytes 12582912 | tf_op jit(solution)/shard_map/mul | solution.py:54
  137.8 4.7 %broadcast_multiply_fusion.3 = (f32[2,256,512]{2,1,0:T(8,128)S(1)}, f32[2,256,512]{2,1,0:T(8,128)S(1)}) fusion(f32[256,512]{1,0:T(8,128)S(1)} %copy-done, f32[2,256,512]{2,1,0:T(8,128)S(1)} %get-tuple-element.18, f32[2,256,512]{2,1,0:T(8,128)} %get-tuple-element.23, f32[2,256,512]{2,1,0:T(8,128)} %get-tuple-element.24, ...), kind=kLoop, calls=%fused_computation.227 | loop fusion | flops 2883584 | bytes 7340032 | tf_op jit(solution)/shard_map/mul | solution.py:54
  142.6 5.0 %fusion.42 = f32[2,256,512]{2,1,0:T(8,128)} fusion(f32[2,256,512]{2,1,0:T(8,128)S(1)} %copy-done.4, f32[2,256,512]{2,1,0:T(8,128)S(1)} %get-tuple-element.11, f32[2,256,512]{2,1,0:T(8,128)S(1)} %copy-done.6, f32[2,256,512]{2,1,0:T(8,128)S(1)} %copy-done.21, f32[2,256,512]{2,1,0:T(8,128)} %get-tuple-element.6, f32[2,256,512]{2,1,0:T(8,128)S(1)} %get-tuple-element.19, ...), kind=kLoop, calls=%fused_computation.94 | loop fusion | flops 9175040 | bytes 16252928 | tf_op jit(solution)/shard_map/add | solution.py:112
  147.8 16.3 %all-reduce.22.cloned.1.call-done = f32[2,256,512]{2,1,0:T(8,128)} async-done(((f32[2,256,512]{2,1,0:T(8,128)}), f32[2,256,512]{2,1,0:T(8,128)}) %all-reduce.22.cloned.1.call-update) | async-done | bytes 1048592 | tf_op jit(solution)/shard_map/psum | solution.py:114
  164.1 1.9 %subtract_multiply_fusion = f32[2,128,512]{2,1,0:T(8,128)} fusion(f32[2,128,512]{2,1,0:T(8,128)S(1)} %copy-done.23, f32[2,256,512]{2,1,0:T(8,128)} %all-reduce.22.cloned.1.call-done, s32[]{:T(128)S(6)} %select_n.236, f32[2,128]{1,0:T(2,128)S(1)} %compare_convert_fusion.2), kind=kLoop, calls=%fused_computation.223 | loop fusion | flops 262144 | bytes 1573892 | tf_op jit(solution)/shard_map/mul | solution.py:118
  (156 shorter events, 27.3 us)
Async XLA Ops:
  6.5 157.5 %all-reduce.22.cloned.1.call-start = ((), (), s32[]{:S(2)}) async-start(), calls=%async_computation | async-start | bytes 2097152 | tf_op jit(solution)/shard_map/psum | solution.py:114
  7.5 17.4 %collective-permute-start.15 = (f32[2,16,512]{2,1,0:T(8,128)S(1)}, f32[2,16,512]{2,1,0:T(8,128)S(1)}, u32[]{:S(2)}, u32[]{:S(2)}) collective-permute-start(f32[2,16,512]{2,1,0:T(8,128)S(1)} %get-tuple-element.32), channel_id=1, source_target_pairs={{0,1},{1,2},{2,3},{3,4},{4,5},{5,6},{6,7},{7,8},{8,9},{9,10},{10,1... | collective-permute-start | bytes 196616 | tf_op jit(solution)/shard_map/ppermute | solution.py:86
  10.5 14.5 %collective-permute-start.16 = (f32[2,16,512]{2,1,0:T(8,128)S(1)}, f32[2,16,512]{2,1,0:T(8,128)S(1)}, u32[]{:S(2)}, u32[]{:S(2)}) collective-permute-start(f32[2,16,512]{2,1,0:T(8,128)S(1)} %get-tuple-element.32), channel_id=1, source_target_pairs={{0,15},{1,0},{2,1},{3,2},{4,3},{5,4},{6,5},{7,6},{8,7},{9,8},{10,9... | collective-permute-start | bytes 196616 | tf_op jit(solution)/shard_map/ppermute | solution.py:91
  14.6 16.0 %collective-permute-start = (f32[2,16,512]{2,1,0:T(8,128)S(1)}, f32[2,16,512]{2,1,0:T(8,128)S(1)}, u32[]{:S(2)}, u32[]{:S(2)}) collective-permute-start(f32[2,16,512]{2,1,0:T(8,128)S(1)} %get-tuple-element.33), channel_id=1, source_target_pairs={{0,1},{1,2},{2,3},{3,4},{4,5},{5,6},{6,7},{7,8},{8,9},{9,10},{10,1... | collective-permute-start | bytes 196616 | tf_op jit(solution)/shard_map/ppermute | solution.py:86
  14.6 16.0 %collective-permute-start.1 = (f32[2,16,512]{2,1,0:T(8,128)S(1)}, f32[2,16,512]{2,1,0:T(8,128)S(1)}, u32[]{:S(2)}, u32[]{:S(2)}) collective-permute-start(f32[2,16,512]{2,1,0:T(8,128)S(1)} %get-tuple-element.33), channel_id=1, source_target_pairs={{0,15},{1,0},{2,1},{3,2},{4,3},{5,4},{6,5},{7,6},{8,7},{9,8},{10,9... | collective-permute-start | bytes 196616 | tf_op jit(solution)/shard_map/ppermute | solution.py:91
  25.0 12.6 %collective-permute-start.18 = (f32[2,16,512]{2,1,0:T(8,128)S(1)}, f32[2,16,512]{2,1,0:T(8,128)S(1)}, u32[]{:S(2)}, u32[]{:S(2)}) collective-permute-start(f32[2,16,512]{2,1,0:T(8,128)S(1)} %collective-permute-done.16), channel_id=1, source_target_pairs={{0,15},{1,0},{2,1},{3,2},{4,3},{5,4},{6,5},{7,6},{8,7},{9,8},{10,9... | collective-permute-start | bytes 196616 | tf_op jit(solution)/shard_map/ppermute | solution.py:91
  30.6 12.6 %collective-permute-start.2 = (f32[2,16,512]{2,1,0:T(8,128)S(1)}, f32[2,16,512]{2,1,0:T(8,128)S(1)}, u32[]{:S(2)}, u32[]{:S(2)}) collective-permute-start(f32[2,16,512]{2,1,0:T(8,128)S(1)} %collective-permute-done), channel_id=1, source_target_pairs={{0,1},{1,2},{2,3},{3,4},{4,5},{5,6},{6,7},{7,8},{8,9},{9,10},{10,1... | collective-permute-start | bytes 196616 | tf_op jit(solution)/shard_map/ppermute | solution.py:86
  30.6 12.6 %collective-permute-start.3 = (f32[2,16,512]{2,1,0:T(8,128)S(1)}, f32[2,16,512]{2,1,0:T(8,128)S(1)}, u32[]{:S(2)}, u32[]{:S(2)}) collective-permute-start(f32[2,16,512]{2,1,0:T(8,128)S(1)} %collective-permute-done.1), channel_id=1, source_target_pairs={{0,15},{1,0},{2,1},{3,2},{4,3},{5,4},{6,5},{7,6},{8,7},{9,8},{10,9... | collective-permute-start | bytes 196616 | tf_op jit(solution)/shard_map/ppermute | solution.py:91
  37.5 12.6 %collective-permute-start.19 = (f32[2,16,512]{2,1,0:T(8,128)S(1)}, f32[2,16,512]{2,1,0:T(8,128)S(1)}, u32[]{:S(2)}, u32[]{:S(2)}) collective-permute-start(f32[2,16,512]{2,1,0:T(8,128)S(1)} %collective-permute-done.17), channel_id=1, source_target_pairs={{0,1},{1,2},{2,3},{3,4},{4,5},{5,6},{6,7},{7,8},{8,9},{9,10},{10,1... | collective-permute-start | bytes 196616 | tf_op jit(solution)/shard_map/ppermute | solution.py:86
  37.6 12.6 %collective-permute-start.20 = (f32[2,16,512]{2,1,0:T(8,128)S(1)}, f32[2,16,512]{2,1,0:T(8,128)S(1)}, u32[]{:S(2)}, u32[]{:S(2)}) collective-permute-start(f32[2,16,512]{2,1,0:T(8,128)S(1)} %collective-permute-done.18), channel_id=1, source_target_pairs={{0,15},{1,0},{2,1},{3,2},{4,3},{5,4},{6,5},{7,6},{8,7},{9,8},{10,9... | collective-permute-start | bytes 196616 | tf_op jit(solution)/shard_map/ppermute | solution.py:91
  43.2 12.6 %collective-permute-start.4 = (f32[2,16,512]{2,1,0:T(8,128)S(1)}, f32[2,16,512]{2,1,0:T(8,128)S(1)}, u32[]{:S(2)}, u32[]{:S(2)}) collective-permute-start(f32[2,16,512]{2,1,0:T(8,128)S(1)} %collective-permute-done.2), channel_id=1, source_target_pairs={{0,1},{1,2},{2,3},{3,4},{4,5},{5,6},{6,7},{7,8},{8,9},{9,10},{10,1... | collective-permute-start | bytes 196616 | tf_op jit(solution)/shard_map/ppermute | solution.py:86
  43.2 12.6 %collective-permute-start.5 = (f32[2,16,512]{2,1,0:T(8,128)S(1)}, f32[2,16,512]{2,1,0:T(8,128)S(1)}, u32[]{:S(2)}, u32[]{:S(2)}) collective-permute-start(f32[2,16,512]{2,1,0:T(8,128)S(1)} %collective-permute-done.3), channel_id=1, source_target_pairs={{0,15},{1,0},{2,1},{3,2},{4,3},{5,4},{6,5},{7,6},{8,7},{9,8},{10,9... | collective-permute-start | bytes 196616 | tf_op jit(solution)/shard_map/ppermute | solution.py:91
  50.1 12.6 %collective-permute-start.21 = (f32[2,16,512]{2,1,0:T(8,128)S(1)}, f32[2,16,512]{2,1,0:T(8,128)S(1)}, u32[]{:S(2)}, u32[]{:S(2)}) collective-permute-start(f32[2,16,512]{2,1,0:T(8,128)S(1)} %collective-permute-done.19), channel_id=1, source_target_pairs={{0,1},{1,2},{2,3},{3,4},{4,5},{5,6},{6,7},{7,8},{8,9},{9,10},{10,1... | collective-permute-start | bytes 196616 | tf_op jit(solution)/shard_map/ppermute | solution.py:86
  50.2 12.6 %collective-permute-start.22 = (f32[2,16,512]{2,1,0:T(8,128)S(1)}, f32[2,16,512]{2,1,0:T(8,128)S(1)}, u32[]{:S(2)}, u32[]{:S(2)}) collective-permute-start(f32[2,16,512]{2,1,0:T(8,128)S(1)} %collective-permute-done.20), channel_id=1, source_target_pairs={{0,15},{1,0},{2,1},{3,2},{4,3},{5,4},{6,5},{7,6},{8,7},{9,8},{10,9... | collective-permute-start | bytes 196616 | tf_op jit(solution)/shard_map/ppermute | solution.py:91
  55.8 12.6 %collective-permute-start.6 = (f32[2,16,512]{2,1,0:T(8,128)S(1)}, f32[2,16,512]{2,1,0:T(8,128)S(1)}, u32[]{:S(2)}, u32[]{:S(2)}) collective-permute-start(f32[2,16,512]{2,1,0:T(8,128)S(1)} %collective-permute-done.4), channel_id=1, source_target_pairs={{0,1},{1,2},{2,3},{3,4},{4,5},{5,6},{6,7},{7,8},{8,9},{9,10},{10,1... | collective-permute-start | bytes 196616 | tf_op jit(solution)/shard_map/ppermute | solution.py:86
  55.8 12.6 %collective-permute-start.7 = (f32[2,16,512]{2,1,0:T(8,128)S(1)}, f32[2,16,512]{2,1,0:T(8,128)S(1)}, u32[]{:S(2)}, u32[]{:S(2)}) collective-permute-start(f32[2,16,512]{2,1,0:T(8,128)S(1)} %collective-permute-done.5), channel_id=1, source_target_pairs={{0,15},{1,0},{2,1},{3,2},{4,3},{5,4},{6,5},{7,6},{8,7},{9,8},{10,9... | collective-permute-start | bytes 196616 | tf_op jit(solution)/shard_map/ppermute | solution.py:91
  62.8 12.6 %collective-permute-start.23 = (f32[2,16,512]{2,1,0:T(8,128)S(1)}, f32[2,16,512]{2,1,0:T(8,128)S(1)}, u32[]{:S(2)}, u32[]{:S(2)}) collective-permute-start(f32[2,16,512]{2,1,0:T(8,128)S(1)} %collective-permute-done.21), channel_id=1, source_target_pairs={{0,1},{1,2},{2,3},{3,4},{4,5},{5,6},{6,7},{7,8},{8,9},{9,10},{10,1... | collective-permute-start | bytes 196616 | tf_op jit(solution)/shard_map/ppermute | solution.py:86
  62.8 12.6 %collective-permute-start.24 = (f32[2,16,512]{2,1,0:T(8,128)S(1)}, f32[2,16,512]{2,1,0:T(8,128)S(1)}, u32[]{:S(2)}, u32[]{:S(2)}) collective-permute-start(f32[2,16,512]{2,1,0:T(8,128)S(1)} %collective-permute-done.22), channel_id=1, source_target_pairs={{0,15},{1,0},{2,1},{3,2},{4,3},{5,4},{6,5},{7,6},{8,7},{9,8},{10,9... | collective-permute-start | bytes 196616 | tf_op jit(solution)/shard_map/ppermute | solution.py:91
  68.5 12.6 %collective-permute-start.8 = (f32[2,16,512]{2,1,0:T(8,128)S(1)}, f32[2,16,512]{2,1,0:T(8,128)S(1)}, u32[]{:S(2)}, u32[]{:S(2)}) collective-permute-start(f32[2,16,512]{2,1,0:T(8,128)S(1)} %collective-permute-done.6), channel_id=1, source_target_pairs={{0,1},{1,2},{2,3},{3,4},{4,5},{5,6},{6,7},{7,8},{8,9},{9,10},{10,1... | collective-permute-start | bytes 196616 | tf_op jit(solution)/shard_map/ppermute | solution.py:86
  68.5 12.6 %collective-permute-start.9 = (f32[2,16,512]{2,1,0:T(8,128)S(1)}, f32[2,16,512]{2,1,0:T(8,128)S(1)}, u32[]{:S(2)}, u32[]{:S(2)}) collective-permute-start(f32[2,16,512]{2,1,0:T(8,128)S(1)} %collective-permute-done.7), channel_id=1, source_target_pairs={{0,15},{1,0},{2,1},{3,2},{4,3},{5,4},{6,5},{7,6},{8,7},{9,8},{10,9... | collective-permute-start | bytes 196616 | tf_op jit(solution)/shard_map/ppermute | solution.py:91
  81.1 12.6 %collective-permute-start.10 = (f32[2,16,512]{2,1,0:T(8,128)S(1)}, f32[2,16,512]{2,1,0:T(8,128)S(1)}, u32[]{:S(2)}, u32[]{:S(2)}) collective-permute-start(f32[2,16,512]{2,1,0:T(8,128)S(1)} %collective-permute-done.8), channel_id=1, source_target_pairs={{0,1},{1,2},{2,3},{3,4},{4,5},{5,6},{6,7},{7,8},{8,9},{9,10},{10,1... | collective-permute-start | bytes 196616 | tf_op jit(solution)/shard_map/ppermute | solution.py:86
  81.1 12.6 %collective-permute-start.11 = (f32[2,16,512]{2,1,0:T(8,128)S(1)}, f32[2,16,512]{2,1,0:T(8,128)S(1)}, u32[]{:S(2)}, u32[]{:S(2)}) collective-permute-start(f32[2,16,512]{2,1,0:T(8,128)S(1)} %collective-permute-done.9), channel_id=1, source_target_pairs={{0,15},{1,0},{2,1},{3,2},{4,3},{5,4},{6,5},{7,6},{8,7},{9,8},{10,9... | collective-permute-start | bytes 196616 | tf_op jit(solution)/shard_map/ppermute | solution.py:91
  88.0 12.6 %collective-permute-start.27 = (f32[2,16,512]{2,1,0:T(8,128)S(1)}, f32[2,16,512]{2,1,0:T(8,128)S(1)}, u32[]{:S(2)}, u32[]{:S(2)}) collective-permute-start(f32[2,16,512]{2,1,0:T(8,128)S(1)} %collective-permute-done.25), channel_id=1, source_target_pairs={{0,1},{1,2},{2,3},{3,4},{4,5},{5,6},{6,7},{7,8},{8,9},{9,10},{10,1... | collective-permute-start | bytes 196616 | tf_op jit(solution)/shard_map/ppermute | solution.py:86
  88.1 14.8 %collective-permute-start.28 = (f32[2,16,512]{2,1,0:T(8,128)S(1)}, f32[2,16,512]{2,1,0:T(8,128)S(1)}, u32[]{:S(2)}, u32[]{:S(2)}) collective-permute-start(f32[2,16,512]{2,1,0:T(8,128)S(1)} %collective-permute-done.26), channel_id=1, source_target_pairs={{0,15},{1,0},{2,1},{3,2},{4,3},{5,4},{6,5},{7,6},{8,7},{9,8},{10,9... | collective-permute-start | bytes 196616 | tf_op jit(solution)/shard_map/ppermute | solution.py:91
  (32 other events, 183.9 us)
Sparse Core Ops, SparseCore 0:
  147.7 16.3 all-reduce.21
